TPU v7x, 256 devices: a whole 4x4x8 slice. The times are simulated.
256 devices in a mesh: rep: 32 (over y, z), hx: 8 (over x, core).
Axes of the slice: x: 4, y: 4, z: 8, core: 2. Of those that a mesh axis runs over, the one named last changes fastest.
Arguments:
- stream_in: bfloat16 [768, 6144], P(None, 'rep'), may hold values from -6 to 6
- query: bfloat16 [768, 6144], P('rep', 'hx'), may hold values from -240 to 240
- new_kv: bfloat16 [768, 2, 1024], P('rep', None, 'hx'), may hold values from -6 to 6
- cache: bfloat16 [768, 2, 128, 1024], P('rep', None, None, 'hx'), may hold values from -127 to 127, as said below
- precision: int32 [768, 4], P('rep'), may hold values from 0 to 1
- cache_scale: float32 [768, 2, 4, 8], P('rep', None, None, 'hx'), may hold values from 0.004 to 0.03
- lengths: int32 [768], P('rep'), may hold values from 0 to 128
- w_heads: bfloat16 [6144, 6144], P('hx', 'rep'), may hold values from -0.3125 to 0.3125
- norm_gain: float32 [6144], P('rep'), may hold values from 0.5 to 1.5
- w_router: bfloat16 [6144, 8], P('rep'), may hold values from -0.0390625 to 0.0390625
- expert_choice: int32 [768, 2], replicated, may hold values from 0 to 7, all different within a row; in each aligned block of 768 rows (0 to 767, 768 to 1535, ...) at most 384 rows name the same one
- w_in: bfloat16 [8, 6144, 2, 8192], P('hx', None, None, 'rep'), may hold values from -0.078125 to 0.078125
- w_down: bfloat16 [8, 8192, 6144], P('hx', 'rep'), may hold values from -0.0625 to 0.0625
- mig_dest: int32 [32], replicated, may hold values from 0 to 31, as said below
- mig_req: int32 [32], replicated, may hold values from 0 to 23
- mig_blocks: int32 [32], replicated, may hold values from 1 to 4
Outputs:
- mixed: bfloat16 [768, 6144], P(None, 'rep')
- arrived: bfloat16 [32, 2, 2, 128, 1024], P('rep', None, None, None, 'hx')
Inputs may be any that keep to these rules, and one draw needn't show every extreme that they name: `cache`: in blocks whose precision entry is 1, the stored values are whole numbers. `expert_choice`: each row names two different experts; over all 768 rows no expert is named by more than 384 rows, a bound that some block reaches. `mig_dest`: no replica names itself; no replica is named by more than 2 replicas, and one is named by exactly 2.
All inputs are finite; a program needn't handle non-finite values.
Results may differ from a plain program's by a relative error of at most 0.0065.
Values may be sent and summed in bfloat16 or wider, within the bound.
A program may use at most 128 MiB of HBM per device.

v0:
```python
import jax
import jax.numpy as jnp
from jax import lax
from jax.sharding import PartitionSpec as P

D = 6144
HEAD = 128
GROUP = 6
BLOCK_LEN = 32
IN_MOST = 2
CACHE = 128
EPSILON = 1e-05


def from_everyone(x, axis):
    copies = jnp.broadcast_to(x, (lax.axis_size(axis), *x.shape))
    return lax.all_to_all(copies, axis, split_axis=0, concat_axis=0, tiled=True)


def in_order(blocks, dim):
    blocks = jnp.moveaxis(blocks, 0, dim)
    lengths = blocks.shape
    return blocks.reshape(*lengths[:dim], lengths[dim] * lengths[dim + 1], *lengths[dim + 2 :])


def gather_directly(x, axis, dim):
    blocks = from_everyone(x, axis)
    return in_order(blocks, dim)


def taken_together(x, axis):
    return from_everyone(x, axis).sum(axis=0)


def over_copies(x, axis):
    everything = from_everyone(x, axis)
    return jnp.sum(everything.astype(jnp.float32), axis=0)


def block_factor(precision, cache_scale):
    factor = jnp.where(precision[:, None, :, None] == 1, cache_scale, 1.0)
    return jnp.repeat(factor, BLOCK_LEN, axis=2)


def attend(query, new_kv, cache, factor, lengths):
    rows = query.shape[0]
    heads_kv = new_kv.shape[2] // HEAD
    scale = HEAD ** (-0.5)
    queries = query.reshape(rows, heads_kv, GROUP, HEAD)
    keys = cache[:, 0].reshape(rows, CACHE, heads_kv, HEAD)
    values = cache[:, 1].reshape(rows, CACHE, heads_kv, HEAD)
    fresh = new_kv.reshape(rows, 2, heads_kv, HEAD)
    scores = jnp.einsum("rkgd,rpkd->rkgp", queries, keys, preferred_element_type=jnp.float32)
    scores = scores * jnp.transpose(factor[:, 0], (0, 2, 1))[:, :, None, :] * scale
    own = (
        jnp.einsum("rkgd,rkd->rkg", queries, fresh[:, 0], preferred_element_type=jnp.float32)
        * scale
    )
    live = jnp.arange(CACHE)[None, :] < lengths[:, None]
    scores = jnp.where(live[:, None, None, :], scores, -jnp.inf)
    top = jnp.maximum(jnp.max(scores, axis=3), own)
    weights = jnp.exp(scores - top[..., None])
    own_weight = jnp.exp(own - top)
    total = jnp.sum(weights, axis=3) + own_weight
    value_weight = (
        weights / total[..., None] * jnp.transpose(factor[:, 1], (0, 2, 1))[:, :, None, :]
    ).astype(jnp.bfloat16)
    own_prob = (own_weight / total).astype(jnp.bfloat16)
    result = jnp.einsum("rkgp,rpkd->rkgd", value_weight, values, preferred_element_type=jnp.float32)
    result = result + own_prob.astype(jnp.float32)[..., None] * fresh[:, 1][:, :, None, :].astype(
        jnp.float32
    )
    return result.reshape(rows, heads_kv * GROUP * HEAD).astype(jnp.bfloat16)


def local(
    stream_in,
    query,
    new_kv,
    cache,
    precision,
    cache_scale,
    lengths,
    w_heads,
    norm_gain,
    w_router,
    expert_choice,
    w_in,
    w_down,
    mig_dest,
    mig_req,
    mig_blocks,
):
    tokens = stream_in.shape[0]
    capacity = tokens // 2
    experts_all = w_router.shape[1]
    factor = block_factor(precision, cache_scale)
    attended = attend(query, new_kv, cache, factor, lengths)
    partial_value = jnp.dot(
        gather_directly(attended, "rep", 0), w_heads, preferred_element_type=jnp.float32
    )
    hidden_state = stream_in.astype(jnp.float32) + taken_together(partial_value, "hx")
    scaled = hidden_state * norm_gain[None, :]
    router_f32 = w_router.astype(jnp.float32)
    squares = taken_together(jnp.sum(hidden_state * hidden_state, axis=1), "rep")
    inverse = lax.rsqrt(squares / D + EPSILON)
    normed = scaled * inverse[:, None]
    logits = taken_together(jnp.dot(normed, router_f32, precision=lax.Precision.HIGHEST), "rep")
    onehot_choice = expert_choice[:, :, None] == jnp.arange(experts_all)[None, None, :]
    chosen = jnp.sum(jnp.where(onehot_choice, logits[:, None, :], 0.0), axis=2)
    peak = jnp.max(chosen, axis=1, keepdims=True)
    expo = jnp.exp(chosen - peak)
    gates = expo / jnp.sum(expo, axis=1, keepdims=True)
    u_rows = normed.astype(jnp.bfloat16)
    expert = lax.axis_index("hx")
    flat = expert_choice.reshape(-1)
    pair_token = jnp.arange(2 * tokens) // 2
    gate_flat = gates.reshape(-1)
    onehot = (flat[:, None] == jnp.arange(experts_all)[None, :]).astype(jnp.int32)
    rank = jnp.sum((jnp.cumsum(onehot, axis=0) - onehot) * onehot, axis=1)
    select = (flat[None, :] == expert) & (rank[None, :] == jnp.arange(capacity)[:, None])
    token_of_slot = jnp.sum(jnp.where(select, pair_token[None, :], 0), axis=1)
    live = jnp.any(select, axis=1)
    gate_of_slot = jnp.sum(jnp.where(select, gate_flat[None, :], 0.0), axis=1)
    match = (token_of_slot[:, None] == jnp.arange(tokens)[None, :]) & live[:, None]
    combine = jnp.where(match, gate_of_slot[:, None], 0.0)
    ff_local = w_in.shape[3]
    w_flat = w_in[0].reshape(D, 2 * ff_local)
    picked = jnp.where(live[:, None], u_rows[token_of_slot], jnp.zeros((), jnp.bfloat16))
    gate_up = jnp.dot(
        lax.all_gather(picked, "rep", axis=1, tiled=True),
        w_flat,
        preferred_element_type=jnp.float32,
    )
    act = (jax.nn.silu(gate_up[:, :ff_local]) * gate_up[:, ff_local:]).astype(jnp.bfloat16)
    down_rows = lax.all_to_all(w_down, "rep", split_axis=2, concat_axis=1, tiled=True)[0]
    expert_out = lax.dot_general(
        down_rows,
        lax.all_gather(act, "rep", axis=1, tiled=True),
        (((0,), (1,)), ((), ())),
        preferred_element_type=jnp.float32,
    )
    weighted = jnp.dot(expert_out, combine, precision=lax.Precision.HIGHEST)
    moe = over_copies(weighted.astype(jnp.bfloat16), "hx").astype(jnp.float32)
    mixed = (hidden_state + moe.T).astype(jnp.bfloat16)
    replica_id = lax.axis_index("rep")
    chosen_req = mig_req[replica_id]
    count = mig_blocks[replica_id]
    levels = lax.dynamic_index_in_dim(cache, chosen_req, 0, keepdims=False).astype(jnp.float32)
    scales = lax.dynamic_index_in_dim(factor, chosen_req, 0, keepdims=False)
    keep = jnp.arange(CACHE) < count * BLOCK_LEN
    outgoing = (
        jnp.where(keep[None, :, None], levels * scales, 0.0).astype(jnp.bfloat16).reshape(1, -1)
    )
    aimed = (mig_dest == replica_id).astype(jnp.int32)
    before = jnp.cumsum(aimed) - aimed
    slots = ((aimed[None, :] == 1) & (before[None, :] == jnp.arange(IN_MOST)[:, None])).astype(
        jnp.bfloat16
    )
    replicas = lax.axis_size("rep")
    target = mig_dest[replica_id]
    outbox = jnp.where(
        (jnp.arange(replicas) == target)[:, None], outgoing, jnp.zeros((), jnp.bfloat16)
    )
    received = lax.all_to_all(outbox, "rep", split_axis=0, concat_axis=0, tiled=True)
    arrived = jnp.dot(slots, received, preferred_element_type=jnp.float32)
    arrived = arrived.astype(jnp.bfloat16).reshape(1, IN_MOST, 2, CACHE, -1)
    return (mixed, arrived)


def solution(mesh):
    placed = (
        P(None, "rep"),
        P("rep", "hx"),
        P("rep", None, "hx"),
        P("rep", None, None, "hx"),
        P("rep", None),
        P("rep", None, None, "hx"),
        P("rep"),
        P("hx", "rep"),
        P("rep"),
        P("rep", None),
        P(),
        P("hx", None, None, "rep"),
        P("hx", "rep", None),
        P(),
        P(),
        P(),
    )
    return jax.shard_map(
        local,
        mesh=mesh,
        in_specs=placed,
        out_specs=(P(None, "rep"), P("rep", None, None, None, "hx")),
        check_vma=False,
    )
```

profile of v0, /device:TPU:1, one launch (start us, length us, event | category | flops | bytes accessed | tf_op | source)
XLA Modules:
  0.0 459.4 jit_solution(9098578894899218675)
XLA Ops:
  7.2 0.7 broadcast_compare_fusion.1
  7.9 0.7 broadcast_select_fusion.2
  8.9 0.8 reshape.308
  9.8 0.7 iota_compare_fusion.5
  10.5 0.7 copy.125
  11.4 1.7 fusion.56
  13.3 1.5 fusion.12
  15.0 43.0 %all_to_all.50 = bf16[32,24,768]{2,1,0:T(8,128)(2,1)S(1)} all-to-all(bf16[32,24,768]{2,1,0:T(8,128)(2,1)S(1)} %broadcast_in_dim.173), channel_id=1, replica_groups=mesh['rep'=32,'hx'=8] {'rep'}, dimensions={0} | all-to-all | bytes 2359296 | tf_op jit(solution)/shard_map/all_to_all | solution.py:17
  58.6 2.6 broadcast_in_dim.174
  61.1 7.3 %all-to-all-start.1 = ((f32[8,768,192]{1,2,0:T(8,128)}), f32[8,768,192]{1,2,0:T(8,128)}, u32[]{:S(2)}, u32[]{:S(2)}) async-start(f32[8,768,192]{1,2,0:T(8,128)} %broadcast_in_dim.174), calls=%async_computation.1 | async-start | bytes 9437184 | tf_op jit(solution)/shard_map/all_to_all | solution.py:17
  69.3 2.3 reduce-window.19
  72.7 50.1 %all-to-all-done.1 = f32[8,768,192]{1,2,0:T(8,128)} async-done(((f32[8,768,192]{1,2,0:T(8,128)}), f32[8,768,192]{1,2,0:T(8,128)}, u32[]{:S(2)}, u32[]{:S(2)}) %all-to-all-start.1) | async-done | bytes 4718624 | tf_op jit(solution)/shard_map/all_to_all | solution.py:17
  122.8 2.7 reduce_sum.102
  126.0 0.7 broadcast_in_dim.176
  126.7 3.9 all-to-all-start.2
  131.0 8.6 %all-to-all-done.2 = f32[32,1,768]{2,1,0:T(1,128)S(1)} async-done(((f32[32,1,768]{2,1,0:T(1,128)}), f32[32,1,768]{2,1,0:T(1,128)S(1)}, u32[]{:S(2)}, u32[]{:S(2)}) %all-to-all-start.2) | async-done | bytes 98336 | tf_op jit(solution)/shard_map/all_to_all | solution.py:17
  139.9 2.1 gather_fusion
  142.1 0.8 copy.93
  142.9 14.0 %copy.94 = bf16[1,256,6144]{1,0,2:T(2,128)(2,1)} copy(bf16[1,256,6144]{2,1,0:T(8,128)(2,1)} %param.28) | data formatting | bytes 6291456 | tf_op args[12]
  157.3 33.3 %reduce.10 = bf16[6144,256]{1,0:T(8,128)(2,1)} reduce(bf16[6144,1,256]{2,1,0:T(2,128)(2,1)} %bitcast.106, bf16[]{:T(256)} %broadcast.197), dimensions={1}, to_apply=%bitcast.88.reduce_sub_computation | reduce | bytes 6291458
  190.6 7.8 %reshape.333 = bf16[32,2,24576]{2,1,0:T(2,128)(2,1)} reshape(bf16[6144,256]{1,0:T(8,128)(2,1)} %reduce.10) | data formatting | bytes 6291456
  198.5 4.8 %all-to-all-start.3 = ((bf16[32,2,24576]{2,1,0:T(2,128)(2,1)}), bf16[32,2,24576]{2,1,0:T(2,128)(2,1)}, u32[]{:S(2)}, u32[]{:S(2)}) async-start(bf16[32,2,24576]{2,1,0:T(2,128)(2,1)} %reshape.333), calls=%async_computation.3 | async-start | bytes 6291456 | tf_op jit(solution)/shard_map/all_to_all | solution.py:136
  203.5 6.6 %copy.109 = bf16[768,8,2,256]{3,1,2,0:T(8,128)(2,1)} copy(bf16[768,8,2,256]{3,2,1,0:T(2,128)(2,1)} %bitcast.109) | data formatting | bytes 12582912
  210.1 28.7 %all-gather.3.cloned.1.call-done = bf16[384,6144]{0,1:T(8,128)(2,1)} async-done(((bf16[384,192]{0,1:T(8,128)(2,1)}), bf16[384,6144]{0,1:T(8,128)(2,1)}) %all-gather.3.cloned.1.call-update) | async-done | bytes 4718608 | tf_op jit(solution)/shard_map/all_gather | solution.py:131
  238.8 6.3 %fusion.58 = f32[384,512]{1,0:T(8,128)S(1)} fusion(bf16[384,6144]{0,1:T(8,128)(2,1)} %all-gather.3.cloned.1.call-done, bf16[6144,512]{1,0:T(8,128)(2,1)} %bitcast.105), kind=kOutput, calls=%fused_computation.109 | convolution fusion | flops 2415919104 | bytes 11796480 | tf_op jit(solution)/shard_map/dot_general | solution.py:130
  245.1 0.8 fusion.24
  250.9 0.9 constant_dynamic-slice_fusion.1
  252.7 34.1 %all-to-all-done.3 = bf16[32,2,24576]{2,1,0:T(2,128)(2,1)} async-done(((bf16[32,2,24576]{2,1,0:T(2,128)(2,1)}), bf16[32,2,24576]{2,1,0:T(2,128)(2,1)}, u32[]{:S(2)}, u32[]{:S(2)}) %all-to-all-start.3) | async-done | bytes 3145760 | tf_op jit(solution)/shard_map/all_to_all | solution.py:136
  286.7 1.0 broadcast_in_dim.180
  287.7 6.6 %all-to-all-start.4 = ((f32[32,768,8]{1,2,0:T(8,128)}), f32[32,768,8]{1,2,0:T(8,128)S(1)}, u32[]{:S(2)}, u32[]{:S(2)}) async-start(f32[32,768,8]{1,2,0:T(8,128)} %broadcast_in_dim.180), calls=%async_computation.4 | async-start | bytes 1572864 | tf_op jit(solution)/shard_map/all_to_all | solution.py:17
  294.3 5.7 %broadcast_select_fusion = bf16[32,1,32768]{2,1,0:T(2,128)(2,1)} fusion(pred[32]{0:T(512)(128)(4,1)S(1)} %iota_compare_fusion.7, bf16[32768]{0:T(1024)(128)(2,1)S(1)} %fusion.28), kind=kLoop, calls=%fused_computation.2 | loop fusion | flops 1048576 | bytes 2162720 | tf_op jit(solution)/shard_map/jit(_where)/select_n | solution.py:162
  299.9 14.4 %reduce.11 = bf16[32,32768]{1,0:T(8,128)(2,1)} reduce(bf16[32,1,32768]{2,1,0:T(2,128)(2,1)} %broadcast_select_fusion, bf16[]{:T(256)} %broadcast.197), dimensions={1}, to_apply=%broadcast_select_fusion.reduce_sub_computation | reduce | bytes 4194306 | tf_op jit(solution)/shard_map/jit(_where)/select_n | solution.py:162
  314.4 4.5 reshape.335
  318.9 9.6 %all-to-all-start.6 = ((bf16[32,2,16384]{2,1,0:T(2,128)(2,1)}), bf16[32,2,16384]{2,1,0:T(2,128)(2,1)}, u32[]{:S(2)}, u32[]{:S(2)}) async-start(bf16[32,2,16384]{2,1,0:T(2,128)(2,1)} %reshape.335), calls=%async_computation.6 | async-start | bytes 4194304 | tf_op jit(solution)/shard_map/all_to_all | solution.py:165
  328.5 19.0 %reshape.334 = bf16[6144,1,256]{2,1,0:T(2,128)(2,1)} reshape(bf16[32,2,24576]{2,1,0:T(2,128)(2,1)} %all-to-all-done.3) | data formatting | bytes 6291456
  347.5 3.4 copy.102
  350.8 2.1 copy.110
  354.0 50.7 %all-gather.5.cloned.1.call-done = bf16[384,8192]{1,0:T(8,128)(2,1)} async-done(((bf16[384,256]{1,0:T(8,128)(2,1)}), bf16[384,8192]{1,0:T(8,128)(2,1)}) %all-gather.5.cloned.1.call-update) | async-done | bytes 6291472 | tf_op jit(solution)/shard_map/all_gather | solution.py:139
  404.7 5.9 %fusion.59 = f32[384,192]{0,1:T(8,128)S(1)} fusion(bf16[384,8192]{1,0:T(8,128)(2,1)} %all-gather.5.cloned.1.call-done, bf16[8192,192]{0,1:T(8,128)(2,1)} %bitcast.111), kind=kOutput, calls=%fused_computation.110 | convolution fusion | flops 1207959552 | bytes 9732096 | tf_op jit(solution)/shard_map/dot_general | solution.py:137
  410.6 1.4 convolution_convert_fusion.1
  412.0 1.6 broadcast_in_dim.187
  413.7 6.4 %all-to-all-start.5 = ((bf16[8,192,768]{2,1,0:T(8,128)(2,1)}), bf16[8,192,768]{2,1,0:T(8,128)(2,1)}, u32[]{:S(2)}, u32[]{:S(2)}) async-start(bf16[8,192,768]{2,1,0:T(8,128)(2,1)} %broadcast_in_dim.187), calls=%async_computation.5 | async-start | bytes 4718592 | tf_op jit(solution)/shard_map/all_to_all | solution.py:17
  420.4 10.5 %reshape.336 = bf16[32,1,32768]{2,1,0:T(2,128)(2,1)} reshape(bf16[32,2,16384]{2,1,0:T(2,128)(2,1)} %all-to-all-done.6) | data formatting | bytes 4194304
  430.8 4.5 fusion.7
  435.3 0.7 copy.111
  436.0 13.2 %all-to-all-done.5 = bf16[8,192,768]{2,1,0:T(8,128)(2,1)} async-done(((bf16[8,192,768]{2,1,0:T(8,128)(2,1)}), bf16[8,192,768]{2,1,0:T(8,128)(2,1)}, u32[]{:S(2)}, u32[]{:S(2)}) %all-to-all-start.5) | async-done | bytes 2359328 | tf_op jit(solution)/shard_map/all_to_all | solution.py:17
  449.2 2.1 convert_reduce_fusion
  451.7 0.9 copy.99
  (83 shorter events, 10.4 us)
Async XLA Ops:
  7.2 50.8 %copy-start = (bf16[768,192]{0,1:T(8,128)(2,1)S(1)}, bf16[768,192]{0,1:T(8,128)(2,1)}, u32[]{:S(2)}) copy-start(bf16[768,192]{0,1:T(8,128)(2,1)} %param.23) | copy-start | bytes 884740
  61.1 7.3 %copy-start.3 = (s32[768,2]{0,1:T(2,128)S(1)}, s32[768,2]{0,1:T(2,128)}, u32[]{:S(2)}) copy-start(s32[768,2]{0,1:T(2,128)} %param.26) | copy-start | bytes 18436
  61.1 7.9 %copy-start.2 = (bf16[768,192]{0,1:T(8,128)(2,1)S(1)}, bf16[768,192]{0,1:T(8,128)(2,1)}, u32[]{:S(2)}) copy-start(bf16[768,192]{0,1:T(8,128)(2,1)} %param.16) | copy-start | bytes 884740
  61.1 61.7 %all-to-all-start.1 = ((f32[8,768,192]{1,2,0:T(8,128)}), f32[8,768,192]{1,2,0:T(8,128)}, u32[]{:S(2)}, u32[]{:S(2)}) async-start(f32[8,768,192]{1,2,0:T(8,128)} %broadcast_in_dim.174), calls=%async_computation.1 | async-start | bytes 9437184 | tf_op jit(solution)/shard_map/all_to_all | solution.py:17
  125.5 14.1 %copy-start.5 = (f32[192]{0:T(256)S(1)}, f32[192]{0:T(256)}, u32[]{:S(2)}) copy-start(f32[192]{0:T(256)} %param.24) | copy-start | bytes 2308
  126.7 12.9 %all-to-all-start.2 = ((f32[32,1,768]{2,1,0:T(1,128)}), f32[32,1,768]{2,1,0:T(1,128)S(1)}, u32[]{:S(2)}, u32[]{:S(2)}) async-start(f32[32,1,768]{2,1,0:T(1,128)} %broadcast_in_dim.176), calls=%async_computation.2 | async-start | bytes 196608 | tf_op jit(solution)/shard_map/all_to_all | solution.py:17
  130.6 108.2 %all-gather.3.cloned.1.call-start = ((), (), s32[]{:S(2)}) async-start(), calls=%async_computation.7 | async-start | bytes 4866048 | tf_op jit(solution)/shard_map/all_gather | solution.py:131
  198.5 88.2 %all-to-all-start.3 = ((bf16[32,2,24576]{2,1,0:T(2,128)(2,1)}), bf16[32,2,24576]{2,1,0:T(2,128)(2,1)}, u32[]{:S(2)}, u32[]{:S(2)}) async-start(bf16[32,2,24576]{2,1,0:T(2,128)(2,1)} %reshape.333), calls=%async_computation.3 | async-start | bytes 6291456 | tf_op jit(solution)/shard_map/all_to_all | solution.py:136
  203.3 201.4 %all-gather.5.cloned.1.call-start = ((), (), s32[]{:S(2)}) async-start(), calls=%async_computation.8 | async-start | bytes 6488064 | tf_op jit(solution)/shard_map/all_gather | solution.py:139
  238.8 7.1 %copy-start.7 = (s32[32]{0:T(128)S(1)}, s32[32]{0:T(128)}, u32[]{:S(2)}) copy-start(s32[32]{0:T(128)} %param.30) | copy-start | bytes 388
  238.8 9.0 %copy-start.8 = (s32[32]{0:T(128)S(1)}, s32[32]{0:T(128)}, u32[]{:S(2)}) copy-start(s32[32]{0:T(128)} %param.31) | copy-start | bytes 388
  238.8 9.7 %copy-start.6 = (s32[32]{0:T(128)S(1)}, s32[32]{0:T(128)}, u32[]{:S(2)}) copy-start(s32[32]{0:T(128)} %param.29) | copy-start | bytes 388
  238.8 13.2 %copy-start.4 = (bf16[192,8]{0,1:T(8,128)(2,1)S(1)}, bf16[192,8]{0,1:T(8,128)(2,1)}, u32[]{:S(2)}) copy-start(bf16[192,8]{0,1:T(8,128)(2,1)} %param.25) | copy-start | bytes 9220
  287.7 31.2 %all-to-all-start.4 = ((f32[32,768,8]{1,2,0:T(8,128)}), f32[32,768,8]{1,2,0:T(8,128)S(1)}, u32[]{:S(2)}, u32[]{:S(2)}) async-start(f32[32,768,8]{1,2,0:T(8,128)} %broadcast_in_dim.180), calls=%async_computation.4 | async-start | bytes 1572864 | tf_op jit(solution)/shard_map/all_to_all | solution.py:17
  318.9 93.1 %all-to-all-start.6 = ((bf16[32,2,16384]{2,1,0:T(2,128)(2,1)}), bf16[32,2,16384]{2,1,0:T(2,128)(2,1)}, u32[]{:S(2)}, u32[]{:S(2)}) async-start(bf16[32,2,16384]{2,1,0:T(2,128)(2,1)} %reshape.335), calls=%async_computation.6 | async-start | bytes 4194304 | tf_op jit(solution)/shard_map/all_to_all | solution.py:165
  413.7 35.5 %all-to-all-start.5 = ((bf16[8,192,768]{2,1,0:T(8,128)(2,1)}), bf16[8,192,768]{2,1,0:T(8,128)(2,1)}, u32[]{:S(2)}, u32[]{:S(2)}) async-start(bf16[8,192,768]{2,1,0:T(8,128)(2,1)} %broadcast_in_dim.187), calls=%async_computation.5 | async-start | bytes 4718592 | tf_op jit(solution)/shard_map/all_to_all | solution.py:17
  449.2 3.4 copy-start.1
Sparse Core Ops, SparseCore 0:
  143.0 95.7 all-gather.2
  246.0 158.6 all-gather.4
where the time goes:
time: 462 us; the launch traced here: 459 us
  waiting for transfers between devices  185 us (40%)
  local copies, waits for them, and re-layouts  85.5 us (19%)
  other arithmetic  67.1 us (15%)
  blocking collectives  43 us (9%)
  starting transfers between devices  38.8 us (8%)
  matrix products  22.7 us (5%)
  between operations  17 us (4%)
    all_to_all x4, waiting for transfers between devices, from_everyone(): return lax.all_to_all(copies, axis, split_axis=0, concat_axis=0, tiled=True)  71.9 us
    unnamed x33, local copies, waits for them, and re-layouts  71 us
    all_gather x1, waiting for transfers between devices, local(): lax.all_gather(act, 'rep', axis=1, tiled=True)  50.7 us
    all_to_all x1, blocking collectives, from_everyone(): return lax.all_to_all(copies, axis, split_axis=0, concat_axis=0, tiled=True)  43 us
    all_to_all x1, waiting for transfers between devices, local(): lax.all_to_all(w_down, 'rep', split_axis=2, concat_axis=1, tiled=True)[0]  34.1 us
    unnamed x2, other arithmetic  33.4 us
    all_gather x1, waiting for transfers between devices, local(): lax.all_gather(picked, 'rep', axis=1, tiled=True)  28.7 us
    all_to_all x4, starting transfers between devices, from_everyone(): return lax.all_to_all(copies, axis, split_axis=0, concat_axis=0, tiled=True)  24.1 us
  transfers between devices with their start and end apart: 8, of which 6 were waited for; matrix products, arithmetic and copies ran while one was open for 33% of the time, Pallas kernels for 0%

commit v1 on v0

--- a/solution.py
+++ b/solution.py
@@ -128,7 +128,9 @@
     w_flat = w_in[0].reshape(D, 2 * ff_local)
     picked = jnp.where(live[:, None], u_rows[token_of_slot], jnp.zeros((), jnp.bfloat16))
     gate_up = jnp.dot(
-        lax.all_gather(picked, "rep", axis=1, tiled=True),
+        jnp.concatenate(
+            lax.all_to_all(jnp.stack([picked] * lax.axis_size("rep")), "rep", 0, 0), axis=1
+        ),
         w_flat,
         preferred_element_type=jnp.float32,
     )

time: 462 us -> 504 us (1.091)
  waiting for transfers between devices: 185 us -> 220 us
  starting transfers between devices: 38.8 us -> 47.4 us
    all_to_all x0 -> x1, waiting for transfers between devices: none -> 51.7 us  [local(): lax.all_to_all(jnp.stack([picked] * lax.axis_size('rep')), 'rep', 0, 0)]
    all_gather x1 -> x0, waiting for transfers between devices: 28.7 us -> none  [local(): lax.all_gather(picked, 'rep', axis=1, tiled=True)]
    all_to_all x1, waiting for transfers between devices: 34.1 us -> 60.4 us  [local(): lax.all_to_all(w_down, 'rep', split_axis=2, concat_axis=1, tiled=True)[0]]
    all_gather x1, waiting for transfers between devices: 50.7 us -> 33.9 us  [local(): lax.all_gather(act, 'rep', axis=1, tiled=True)]
    all_to_all x0 -> x1, starting transfers between devices: none -> 5.04 us  [local(): lax.all_to_all(jnp.stack([picked] * lax.axis_size('rep')), 'rep', 0, 0)]
  transfers between devices with their start and end apart: 8 -> 8, of which waited for: 6 -> 7; matrix products, arithmetic and copies ran while one was open for 33% -> 30% of each run, Pallas kernels for 0% -> 0%
where the time goes in v1:
time: 504 us; the launch traced here: 501 us
  waiting for transfers between devices  220 us (44%)
  local copies, waits for them, and re-layouts  85 us (17%)
  other arithmetic  67 us (13%)
  starting transfers between devices  47.4 us (9%)
  blocking collectives  43 us (9%)
  matrix products  21.4 us (4%)
  between operations  17 us (3%)
    all_to_all x4, waiting for transfers between devices, from_everyone(): return lax.all_to_all(copies, axis, split_axis=0, concat_axis=0, tiled=True)  74 us
    unnamed x33, local copies, waits for them, and re-layouts  68.1 us
    all_to_all x1, waiting for transfers between devices, local(): lax.all_to_all(w_down, 'rep', split_axis=2, concat_axis=1, tiled=True)[0]  60.4 us
    all_to_all x1, waiting for transfers between devices, local(): lax.all_to_all(jnp.stack([picked] * lax.axis_size('rep')), 'rep', 0, 0)  51.7 us
    all_to_all x1, blocking collectives, from_everyone(): return lax.all_to_all(copies, axis, split_axis=0, concat_axis=0, tiled=True)  43 us
    all_gather x1, waiting for transfers between devices, local(): lax.all_gather(act, 'rep', axis=1, tiled=True)  33.9 us
    unnamed x2, other arithmetic  33.3 us
    all_to_all x4, starting transfers between devices, from_everyone(): return lax.all_to_all(copies, axis, split_axis=0, concat_axis=0, tiled=True)  28.4 us
  transfers between devices with their start and end apart: 8, of which 7 were waited for; matrix products, arithmetic and copies ran while one was open for 30% of the time, Pallas kernels for 0%

profile of v1, /device:TPU:1, one launch (start us, length us, event | category | flops | bytes accessed | tf_op | source)
XLA Modules:
  0.0 501.0 jit_solution(16855401401481794313)
XLA Ops:
  7.2 0.7 broadcast_compare_fusion.1
  8.9 0.8 reshape.322
  9.8 0.7 iota_compare_fusion.5
  10.5 0.7 copy.126
  11.4 1.7 fusion.56
  13.3 1.5 fusion.12
  15.0 43.0 %all_to_all.55 = bf16[32,24,768]{2,1,0:T(8,128)(2,1)S(1)} all-to-all(bf16[32,24,768]{2,1,0:T(8,128)(2,1)S(1)} %broadcast_in_dim.173), channel_id=1, replica_groups=mesh['rep'=32,'hx'=8] {'rep'}, dimensions={0} | all-to-all | bytes 2359296 | tf_op jit(solution)/shard_map/all_to_all | solution.py:17
  58.6 2.6 broadcast_in_dim.174
  61.1 7.3 %all-to-all-start.1 = ((f32[8,768,192]{1,2,0:T(8,128)}), f32[8,768,192]{1,2,0:T(8,128)}, u32[]{:S(2)}, u32[]{:S(2)}) async-start(f32[8,768,192]{1,2,0:T(8,128)} %broadcast_in_dim.174), calls=%async_computation.1 | async-start | bytes 9437184 | tf_op jit(solution)/shard_map/all_to_all | solution.py:17
  69.3 2.3 reduce-window.19
  72.7 50.1 %all-to-all-done.1 = f32[8,768,192]{1,2,0:T(8,128)} async-done(((f32[8,768,192]{1,2,0:T(8,128)}), f32[8,768,192]{1,2,0:T(8,128)}, u32[]{:S(2)}, u32[]{:S(2)}) %all-to-all-start.1) | async-done | bytes 4718624 | tf_op jit(solution)/shard_map/all_to_all | solution.py:17
  122.8 2.7 reduce_sum.102
  126.0 0.7 broadcast_in_dim.176
  126.7 3.9 all-to-all-start.2
  131.0 8.6 %all-to-all-done.2 = f32[32,1,768]{2,1,0:T(1,128)S(1)} async-done(((f32[32,1,768]{2,1,0:T(1,128)}), f32[32,1,768]{2,1,0:T(1,128)S(1)}, u32[]{:S(2)}, u32[]{:S(2)}) %all-to-all-start.2) | async-done | bytes 98336 | tf_op jit(solution)/shard_map/all_to_all | solution.py:17
  139.9 2.1 gather_fusion
  142.2 2.9 stack.2
  145.1 5.0 %all-to-all-start.3 = ((bf16[32,384,192]{1,2,0:T(8,128)(2,1)}), bf16[32,384,192]{1,2,0:T(8,128)(2,1)}, u32[]{:S(2)}, u32[]{:S(2)}) async-start(bf16[32,384,192]{1,2,0:T(8,128)(2,1)} %stack.2), calls=%async_computation.3 | async-start | bytes 9437184 | tf_op jit(solution)/shard_map/all_to_all | solution.py:132
  150.2 14.0 %copy.95 = bf16[1,256,6144]{1,0,2:T(2,128)(2,1)} copy(bf16[1,256,6144]{2,1,0:T(8,128)(2,1)} %param.28) | data formatting | bytes 6291456 | tf_op args[12]
  164.6 33.2 %reduce.10 = bf16[6144,256]{1,0:T(8,128)(2,1)} reduce(bf16[6144,1,256]{2,1,0:T(2,128)(2,1)} %bitcast.109, bf16[]{:T(256)} %broadcast.202), dimensions={1}, to_apply=%bitcast.91.reduce_sub_computation | reduce | bytes 6291458
  197.9 7.8 %reshape.349 = bf16[32,2,24576]{2,1,0:T(2,128)(2,1)} reshape(bf16[6144,256]{1,0:T(8,128)(2,1)} %reduce.10) | data formatting | bytes 6291456
  205.7 51.7 %all-to-all-done.3 = bf16[32,384,192]{1,2,0:T(8,128)(2,1)} async-done(((bf16[32,384,192]{1,2,0:T(8,128)(2,1)}), bf16[32,384,192]{1,2,0:T(8,128)(2,1)}, u32[]{:S(2)}, u32[]{:S(2)}) %all-to-all-start.3) | async-done | bytes 4718624 | tf_op jit(solution)/shard_map/all_to_all | solution.py:132
  257.4 5.9 %all-to-all-start.4 = ((bf16[32,2,24576]{2,1,0:T(2,128)(2,1)}), bf16[32,2,24576]{2,1,0:T(2,128)(2,1)}, u32[]{:S(2)}, u32[]{:S(2)}) async-start(bf16[32,2,24576]{2,1,0:T(2,128)(2,1)} %reshape.349), calls=%async_computation.4 | async-start | bytes 6291456 | tf_op jit(solution)/shard_map/all_to_all | solution.py:138
  263.3 3.8 copy.110
  267.2 5.0 fusion.58
  272.2 0.8 fusion.24
  278.1 0.9 constant_dynamic-slice_fusion.1
  279.8 60.4 %all-to-all-done.4 = bf16[32,2,24576]{2,1,0:T(2,128)(2,1)} async-done(((bf16[32,2,24576]{2,1,0:T(2,128)(2,1)}), bf16[32,2,24576]{2,1,0:T(2,128)(2,1)}, u32[]{:S(2)}, u32[]{:S(2)}) %all-to-all-start.4) | async-done | bytes 3145760 | tf_op jit(solution)/shard_map/all_to_all | solution.py:138
  340.2 1.0 broadcast_in_dim.180
  341.2 9.6 %all-to-all-start.5 = ((f32[32,768,8]{1,2,0:T(8,128)}), f32[32,768,8]{1,2,0:T(8,128)S(1)}, u32[]{:S(2)}, u32[]{:S(2)}) async-start(f32[32,768,8]{1,2,0:T(8,128)} %broadcast_in_dim.180), calls=%async_computation.5 | async-start | bytes 1572864 | tf_op jit(solution)/shard_map/all_to_all | solution.py:17
  350.8 5.7 %broadcast_select_fusion = bf16[32,1,32768]{2,1,0:T(2,128)(2,1)} fusion(pred[32]{0:T(512)(128)(4,1)S(1)} %iota_compare_fusion.7, bf16[32768]{0:T(1024)(128)(2,1)S(1)} %fusion.28), kind=kLoop, calls=%fused_computation.2 | loop fusion | flops 1048576 | bytes 2162720 | tf_op jit(solution)/shard_map/jit(_where)/select_n | solution.py:164
  356.5 14.4 %reduce.11 = bf16[32,32768]{1,0:T(8,128)(2,1)} reduce(bf16[32,1,32768]{2,1,0:T(2,128)(2,1)} %broadcast_select_fusion, bf16[]{:T(256)} %broadcast.202), dimensions={1}, to_apply=%broadcast_select_fusion.reduce_sub_computation | reduce | bytes 4194306 | tf_op jit(solution)/shard_map/jit(_where)/select_n | solution.py:164
  370.9 4.5 reshape.351
  375.5 2.1 all-to-all-done.5
  377.5 8.0 %all-to-all-start.7 = ((bf16[32,2,16384]{2,1,0:T(2,128)(2,1)}), bf16[32,2,16384]{2,1,0:T(2,128)(2,1)}, u32[]{:S(2)}, u32[]{:S(2)}) async-start(bf16[32,2,16384]{2,1,0:T(2,128)(2,1)} %reshape.351), calls=%async_computation.7 | async-start | bytes 4194304 | tf_op jit(solution)/shard_map/all_to_all | solution.py:167
  385.5 19.0 %reshape.350 = bf16[6144,1,256]{2,1,0:T(2,128)(2,1)} reshape(bf16[32,2,24576]{2,1,0:T(2,128)(2,1)} %all-to-all-done.4) | data formatting | bytes 6291456
  404.5 3.3 copy.103
  407.8 2.1 copy.111
  411.0 33.9 %all-gather.2.cloned.1.call-done = bf16[384,8192]{1,0:T(8,128)(2,1)} async-done(((bf16[384,256]{1,0:T(8,128)(2,1)}), bf16[384,8192]{1,0:T(8,128)(2,1)}) %all-gather.2.cloned.1.call-update) | async-done | bytes 6291472 | tf_op jit(solution)/shard_map/all_gather | solution.py:141
  444.9 5.9 %fusion.59 = f32[384,192]{0,1:T(8,128)S(1)} fusion(bf16[384,8192]{1,0:T(8,128)(2,1)} %all-gather.2.cloned.1.call-done, bf16[8192,192]{0,1:T(8,128)(2,1)} %bitcast.114), kind=kOutput, calls=%fused_computation.110 | convolution fusion | flops 1207959552 | bytes 9732096 | tf_op jit(solution)/shard_map/dot_general | solution.py:139
  450.9 1.4 convolution_convert_fusion.1
  452.3 1.6 broadcast_in_dim.187
  453.9 7.7 %all-to-all-start.6 = ((bf16[8,192,768]{2,1,0:T(8,128)(2,1)}), bf16[8,192,768]{2,1,0:T(8,128)(2,1)}, u32[]{:S(2)}, u32[]{:S(2)}) async-start(bf16[8,192,768]{2,1,0:T(8,128)(2,1)} %broadcast_in_dim.187), calls=%async_computation.6 | async-start | bytes 4718592 | tf_op jit(solution)/shard_map/all_to_all | solution.py:17
  461.9 10.5 %reshape.352 = bf16[32,1,32768]{2,1,0:T(2,128)(2,1)} reshape(bf16[32,2,16384]{2,1,0:T(2,128)(2,1)} %all-to-all-done.7) | data formatting | bytes 4194304
  472.3 4.5 fusion.7
  477.5 13.2 %all-to-all-done.6 = bf16[8,192,768]{2,1,0:T(8,128)(2,1)} async-done(((bf16[8,192,768]{2,1,0:T(8,128)(2,1)}), bf16[8,192,768]{2,1,0:T(8,128)(2,1)}, u32[]{:S(2)}, u32[]{:S(2)}) %all-to-all-start.6) | async-done | bytes 2359328 | tf_op jit(solution)/shard_map/all_to_all | solution.py:17
  490.8 2.1 convert_reduce_fusion
  493.3 0.9 copy.100
  (83 shorter events, 11.7 us)
Async XLA Ops:
  7.2 50.8 %copy-start = (bf16[768,192]{0,1:T(8,128)(2,1)S(1)}, bf16[768,192]{0,1:T(8,128)(2,1)}, u32[]{:S(2)}) copy-start(bf16[768,192]{0,1:T(8,128)(2,1)} %param.23) | copy-start | bytes 884740
  61.1 7.3 %copy-start.3 = (s32[768,2]{0,1:T(2,128)S(1)}, s32[768,2]{0,1:T(2,128)}, u32[]{:S(2)}) copy-start(s32[768,2]{0,1:T(2,128)} %param.26) | copy-start | bytes 18436
  61.1 7.9 %copy-start.2 = (bf16[768,192]{0,1:T(8,128)(2,1)S(1)}, bf16[768,192]{0,1:T(8,128)(2,1)}, u32[]{:S(2)}) copy-start(bf16[768,192]{0,1:T(8,128)(2,1)} %param.16) | copy-start | bytes 884740
  61.1 61.7 %all-to-all-start.1 = ((f32[8,768,192]{1,2,0:T(8,128)}), f32[8,768,192]{1,2,0:T(8,128)}, u32[]{:S(2)}, u32[]{:S(2)}) async-start(f32[8,768,192]{1,2,0:T(8,128)} %broadcast_in_dim.174), calls=%async_computation.1 | async-start | bytes 9437184 | tf_op jit(solution)/shard_map/all_to_all | solution.py:17
  125.5 14.1 %copy-start.5 = (f32[192]{0:T(256)S(1)}, f32[192]{0:T(256)}, u32[]{:S(2)}) copy-start(f32[192]{0:T(256)} %param.24) | copy-start | bytes 2308
  126.7 12.9 %all-to-all-start.2 = ((f32[32,1,768]{2,1,0:T(1,128)}), f32[32,1,768]{2,1,0:T(1,128)S(1)}, u32[]{:S(2)}, u32[]{:S(2)}) async-start(f32[32,1,768]{2,1,0:T(1,128)} %broadcast_in_dim.176), calls=%async_computation.2 | async-start | bytes 196608 | tf_op jit(solution)/shard_map/all_to_all | solution.py:17
  145.1 112.3 %all-to-all-start.3 = ((bf16[32,384,192]{1,2,0:T(8,128)(2,1)}), bf16[32,384,192]{1,2,0:T(8,128)(2,1)}, u32[]{:S(2)}, u32[]{:S(2)}) async-start(bf16[32,384,192]{1,2,0:T(8,128)(2,1)} %stack.2), calls=%async_computation.3 | async-start | bytes 9437184 | tf_op jit(solution)/shard_map/all_to_all | solution.py:132
  257.4 82.8 %all-to-all-start.4 = ((bf16[32,2,24576]{2,1,0:T(2,128)(2,1)}), bf16[32,2,24576]{2,1,0:T(2,128)(2,1)}, u32[]{:S(2)}, u32[]{:S(2)}) async-start(bf16[32,2,24576]{2,1,0:T(2,128)(2,1)} %reshape.349), calls=%async_computation.4 | async-start | bytes 6291456 | tf_op jit(solution)/shard_map/all_to_all | solution.py:138
  263.3 181.7 %all-gather.2.cloned.1.call-start = ((), (), s32[]{:S(2)}) async-start(), calls=%async_computation.8 | async-start | bytes 6488064 | tf_op jit(solution)/shard_map/all_gather | solution.py:141
  267.2 5.9 %copy-start.7 = (s32[32]{0:T(128)S(1)}, s32[32]{0:T(128)}, u32[]{:S(2)}) copy-start(s32[32]{0:T(128)} %param.30) | copy-start | bytes 388
  267.2 7.8 %copy-start.8 = (s32[32]{0:T(128)S(1)}, s32[32]{0:T(128)}, u32[]{:S(2)}) copy-start(s32[32]{0:T(128)} %param.31) | copy-start | bytes 388
  267.2 8.4 %copy-start.6 = (s32[32]{0:T(128)S(1)}, s32[32]{0:T(128)}, u32[]{:S(2)}) copy-start(s32[32]{0:T(128)} %param.29) | copy-start | bytes 388
  267.2 11.9 %copy-start.4 = (bf16[192,8]{0,1:T(8,128)(2,1)S(1)}, bf16[192,8]{0,1:T(8,128)(2,1)}, u32[]{:S(2)}) copy-start(bf16[192,8]{0,1:T(8,128)(2,1)} %param.25) | copy-start | bytes 9220
  341.2 36.3 %all-to-all-start.5 = ((f32[32,768,8]{1,2,0:T(8,128)}), f32[32,768,8]{1,2,0:T(8,128)S(1)}, u32[]{:S(2)}, u32[]{:S(2)}) async-start(f32[32,768,8]{1,2,0:T(8,128)} %broadcast_in_dim.180), calls=%async_computation.5 | async-start | bytes 1572864 | tf_op jit(solution)/shard_map/all_to_all | solution.py:17
  377.5 74.8 %all-to-all-start.7 = ((bf16[32,2,16384]{2,1,0:T(2,128)(2,1)}), bf16[32,2,16384]{2,1,0:T(2,128)(2,1)}, u32[]{:S(2)}, u32[]{:S(2)}) async-start(bf16[32,2,16384]{2,1,0:T(2,128)(2,1)} %reshape.351), calls=%async_computation.7 | async-start | bytes 4194304 | tf_op jit(solution)/shard_map/all_to_all | solution.py:167
  453.9 36.8 %all-to-all-start.6 = ((bf16[8,192,768]{2,1,0:T(8,128)(2,1)}), bf16[8,192,768]{2,1,0:T(8,128)(2,1)}, u32[]{:S(2)}, u32[]{:S(2)}) async-start(bf16[8,192,768]{2,1,0:T(8,128)(2,1)} %broadcast_in_dim.187), calls=%async_computation.6 | async-start | bytes 4718592 | tf_op jit(solution)/shard_map/all_to_all | solution.py:17
  490.8 3.4 copy-start.1
Sparse Core Ops, SparseCore 0:
  273.1 171.7 all-gather.1
